TPU v7x, 32 devices: a whole 2x2x4 slice. The times are simulated.
32 devices in a mesh: dp: 4 (over x, core), ctx: 4 (over z), tensor: 2 (over y).
Axes of the slice: x: 2, y: 2, z: 4, core: 2. Of those that a mesh axis runs over, the one named last changes fastest.
Arguments:
- inputs: bfloat16 [8192, 768], P(('dp', 'ctx')), may hold values from -6 to 6
- segments: int32 [4, 2048], P('dp', 'ctx'), may hold values from 0 to 7, never falling along the last dimension, each value on 1 to 1536 neighbouring positions
- query_proj: bfloat16 [768, 768], P(None, 'tensor'), may hold values from -0.4375 to 0.4375
- key_proj: bfloat16 [768, 768], P(None, 'tensor'), may hold values from -0.21875 to 0.21875
- value_proj: bfloat16 [768, 768], P(None, 'tensor'), may hold values from -0.21875 to 0.21875
- query_bias: bfloat16 [768], P('tensor'), may hold values from -3 to 3
- value_bias: bfloat16 [768], P('tensor'), may hold values from -0.59765625 to 0.59765625
- output_proj: bfloat16 [768, 768], P('tensor'), may hold values from -0.875 to 0.875
- output_bias: bfloat16 [768], replicated, may hold values from -1.1953125 to 1.1953125
- attn_gain: bfloat16 [768], replicated, may hold values from 0.5 to 1.5
- attn_shift: bfloat16 [768], replicated, may hold values from -1.1953125 to 1.1953125
- expand_proj: bfloat16 [768, 3072], P(None, 'tensor'), may hold values from -0.21875 to 0.21875
- expand_bias: bfloat16 [3072], P('tensor'), may hold values from -3 to 3
- shrink_proj: bfloat16 [3072, 768], P('tensor'), may hold values from -0.109375 to 0.109375
- shrink_bias: bfloat16 [768], replicated, may hold values from -1.1953125 to 1.1953125
- final_gain: bfloat16 [768], replicated, may hold values from 0.5 to 1.5
- final_shift: bfloat16 [768], replicated, may hold values from -1.1953125 to 1.1953125
- cotangent: bfloat16 [8192, 768], P(('dp', 'ctx')), may hold values from -6 to 6
Outputs:
- output: bfloat16 [8192, 768], P(('dp', 'ctx'))
- input_grad: float32 [8192, 768], P(('dp', 'ctx'))
- query_grad: float32 [768, 768], P(None, 'tensor')
- key_grad: float32 [768, 768], P(None, 'tensor')
- value_grad: float32 [768, 768], P(None, 'tensor')
- qbias_grad: float32 [768], P('tensor')
- vbias_grad: float32 [768], P('tensor')
- oproj_grad: float32 [768, 768], P('tensor')
- obias_grad: float32 [768], replicated
- again_grad: float32 [768], replicated
- ashift_grad: float32 [768], replicated
- expand_grad: float32 [768, 3072], P(None, 'tensor')
- ebias_grad: float32 [3072], P('tensor')
- shrink_grad: float32 [3072, 768], P('tensor')
- sbias_grad: float32 [768], replicated
- fgain_grad: float32 [768], replicated
- fshift_grad: float32 [768], replicated
Inputs may be any that keep to these rules, and one draw needn't show every extreme that they name: `segments`: along each sequence the ids never fall; every id from 0 to 7 names one document of the sequence, and one document has 1536 tokens.
All inputs are finite; a program needn't handle non-finite values.
Results may differ from a plain program's by a relative error of at most 0.019.
Values may be sent and summed in bfloat16 or wider, within the bound.
A program may use at most 256 MiB of HBM per device.

v0:
```python
import jax
import jax.numpy as jnp
from jax import lax
from jax.sharding import PartitionSpec as P

HEAD_DIM = 64
norm_eps = 1e-12
masked = -1e30
contract_rows = (((0,), (0,)), ((), ()))
contract_cols = (((1,), (1,)), ((), ()))


def matmul(left, right):
    return jnp.dot(left, right, preferred_element_type=jnp.float32)


def inner_rows(left, right):
    return lax.dot_general(left, right, contract_rows, preferred_element_type=jnp.float32)


def inner_cols(left, right):
    return lax.dot_general(left, right, contract_cols, preferred_element_type=jnp.float32)


def norm_forward(values, gain, shift):
    centred = values - jnp.mean(values, axis=-1, keepdims=True)
    spread = jnp.mean(centred * centred, axis=-1, keepdims=True)
    recip = lax.rsqrt(spread + norm_eps)
    normed = centred * recip
    return (normed * gain + shift, normed, recip)


def norm_backward(upstream, normed, recip, gain):
    scaled = upstream * gain
    centred = (
        scaled
        - jnp.mean(scaled, axis=-1, keepdims=True)
        - normed * jnp.mean(scaled * normed, axis=-1, keepdims=True)
    )
    return (centred * recip, jnp.sum(upstream * normed, axis=0), jnp.sum(upstream, axis=0))


def cross_scores(left, right):
    return inner_cols(left, right)


def spread_apply(weights_in, right):
    return matmul(weights_in, right)


def spread_transpose(weights_in, left):
    return inner_rows(weights_in, left)


def body(
    inputs,
    segments,
    query_proj,
    key_proj,
    value_proj,
    query_bias,
    value_bias,
    output_proj,
    output_bias,
    attn_gain,
    attn_shift,
    expand_proj,
    expand_bias,
    shrink_proj,
    shrink_bias,
    final_gain,
    final_shift,
    cotangent,
):
    head_count = query_proj.shape[1] // HEAD_DIM
    scale = HEAD_DIM ** (-0.5)
    seg_local = segments[0]
    queries = (matmul(inputs, query_proj) + query_bias.astype(jnp.float32)).astype(jnp.bfloat16)
    keys = matmul(inputs, key_proj).astype(jnp.bfloat16)
    values = (matmul(inputs, value_proj) + value_bias.astype(jnp.float32)).astype(jnp.bfloat16)
    all_keys, all_values, key_ids = (
        lax.all_gather(keys, "ctx", axis=0, tiled=True),
        lax.all_gather(values, "ctx", axis=0, tiled=True),
        lax.all_gather(seg_local.astype(jnp.bfloat16), "ctx", axis=0, tiled=True),
    )
    query_segs = seg_local.astype(jnp.float32)
    key_segs = key_ids.astype(jnp.float32)
    same_seg = query_segs[:, None] == key_segs[None, :]

    def split_heads(matrix):
        return jnp.swapaxes(matrix.reshape(matrix.shape[0], head_count, HEAD_DIM), 0, 1)

    def join_heads(stack):
        return jnp.swapaxes(stack, 0, 1).reshape(stack.shape[1], head_count * HEAD_DIM)

    query_heads = split_heads(queries)
    key_heads = split_heads(all_keys)
    value_heads = split_heads(all_values)

    def head_forward(state, triple):
        query_head, key_head, value_head = triple
        scores = cross_scores(query_head, key_head) * scale
        scores = jnp.where(same_seg, scores, masked)
        row_max = jnp.max(scores, axis=1, keepdims=True)
        exp_scores = jnp.where(same_seg, jnp.exp(scores - row_max), 0.0)
        row_sum = jnp.sum(exp_scores, axis=1, keepdims=True)
        attn_probs = (exp_scores / row_sum).astype(jnp.bfloat16)
        mixed = spread_apply(attn_probs, value_head)
        return (state, (mixed, row_max + jnp.log(row_sum)))

    mixed_heads, log_sums = lax.scan(head_forward, None, (query_heads, key_heads, value_heads))[1]
    attended = join_heads(mixed_heads).astype(jnp.bfloat16)
    attn_total = lax.psum(matmul(attended, output_proj).astype(jnp.bfloat16), "tensor").astype(
        jnp.float32
    )
    attn_gain_f = attn_gain.astype(jnp.float32)
    first, first_normed, first_recip = norm_forward(
        inputs.astype(jnp.float32) + attn_total + output_bias.astype(jnp.float32),
        attn_gain_f,
        attn_shift.astype(jnp.float32),
    )
    first_low = first.astype(jnp.bfloat16)
    pre_act = matmul(first_low, expand_proj) + expand_bias.astype(jnp.float32)
    activated, gelu_back = jax.vjp(lambda pre_in: jax.nn.gelu(pre_in, approximate=False), pre_act)
    hidden = activated.astype(jnp.bfloat16)
    feed_total = lax.psum(matmul(hidden, shrink_proj).astype(jnp.bfloat16), "tensor").astype(
        jnp.float32
    )
    second = first + feed_total + shrink_bias.astype(jnp.float32)
    final_gain_f = final_gain.astype(jnp.float32)
    output, second_normed, second_recip = norm_forward(
        second, final_gain_f, final_shift.astype(jnp.float32)
    )
    upstream = cotangent.astype(jnp.float32)
    grad_second, fgain_grad, fshift_grad = norm_backward(
        upstream, second_normed, second_recip, final_gain_f
    )
    sbias_grad = jnp.sum(grad_second, axis=0)
    grad_second_low = grad_second.astype(jnp.bfloat16)
    shrink_grad = inner_rows(hidden, grad_second_low)
    grad_act = inner_cols(grad_second_low, shrink_proj)
    grad_pre = gelu_back(grad_act)[0].astype(jnp.bfloat16)
    ebias_grad = jnp.sum(grad_pre.astype(jnp.float32), axis=0)
    expand_grad = inner_rows(first_low, grad_pre)
    grad_first = grad_second + lax.psum(
        inner_cols(grad_pre, expand_proj).astype(jnp.bfloat16), "tensor"
    ).astype(jnp.float32)
    grad_mix, again_grad, ashift_grad = norm_backward(
        grad_first, first_normed, first_recip, attn_gain_f
    )
    obias_grad = jnp.sum(grad_mix, axis=0)
    grad_mix_low = grad_mix.astype(jnp.bfloat16)
    oproj_grad = inner_rows(attended, grad_mix_low)
    grad_attended = inner_cols(grad_mix_low, output_proj).astype(jnp.bfloat16)
    grad_heads = split_heads(grad_attended)

    def head_backward(state, group):
        query_head, key_head, value_head, grad_head, log_sum = group
        scores = cross_scores(query_head, key_head) * scale
        attn_probs = jnp.where(same_seg, jnp.exp(scores - log_sum), 0.0)
        grad_probs = cross_scores(grad_head, value_head)
        row_dot = jnp.sum(attn_probs * grad_probs, axis=1, keepdims=True)
        grad_scores = (attn_probs * (grad_probs - row_dot)).astype(jnp.bfloat16)
        grad_query = spread_apply(grad_scores, key_head) * scale
        grad_key = spread_transpose(grad_scores, query_head) * scale
        grad_value = spread_transpose(attn_probs.astype(jnp.bfloat16), grad_head)
        return (state, (grad_query, grad_key, grad_value))

    query_back, key_back, value_back = lax.scan(
        head_backward, None, (query_heads, key_heads, value_heads, grad_heads, log_sums)
    )[1]
    grad_queries = join_heads(query_back).astype(jnp.bfloat16)
    key_sum, value_sum = (
        lax.psum_scatter(
            join_heads(key_back).astype(jnp.bfloat16), "ctx", scatter_dimension=0, tiled=True
        ).astype(jnp.float32),
        lax.psum_scatter(
            join_heads(value_back).astype(jnp.bfloat16), "ctx", scatter_dimension=0, tiled=True
        ).astype(jnp.float32),
    )
    grad_keys = key_sum.astype(jnp.bfloat16)
    grad_values = value_sum.astype(jnp.bfloat16)
    qbias_grad = jnp.sum(grad_queries.astype(jnp.float32), axis=0)
    vbias_grad = jnp.sum(grad_values.astype(jnp.float32), axis=0)
    query_grad = inner_rows(inputs, grad_queries)
    key_grad = inner_rows(inputs, grad_keys)
    value_grad = inner_rows(inputs, grad_values)
    back_terms = (
        inner_cols(grad_queries, query_proj)
        + inner_cols(grad_keys, key_proj)
        + inner_cols(grad_values, value_proj)
    )
    input_grad = grad_mix + lax.psum(back_terms.astype(jnp.bfloat16), "tensor").astype(jnp.float32)
    (
        query_grad,
        key_grad,
        value_grad,
        qbias_grad,
        vbias_grad,
        oproj_grad,
        obias_grad,
        again_grad,
        ashift_grad,
        expand_grad,
        ebias_grad,
        shrink_grad,
        sbias_grad,
        fgain_grad,
        fshift_grad,
    ) = lax.psum(
        (
            query_grad,
            key_grad,
            value_grad,
            qbias_grad,
            vbias_grad,
            oproj_grad,
            obias_grad,
            again_grad,
            ashift_grad,
            expand_grad,
            ebias_grad,
            shrink_grad,
            sbias_grad,
            fgain_grad,
            fshift_grad,
        ),
        ("dp", "ctx"),
    )
    return (
        output.astype(jnp.bfloat16),
        input_grad,
        query_grad,
        key_grad,
        value_grad,
        qbias_grad,
        vbias_grad,
        oproj_grad,
        obias_grad,
        again_grad,
        ashift_grad,
        expand_grad,
        ebias_grad,
        shrink_grad,
        sbias_grad,
        fgain_grad,
        fshift_grad,
    )


def solution(mesh):
    in_specs = (
        P(("dp", "ctx"), None),
        P("dp", "ctx"),
        P(None, "tensor"),
        P(None, "tensor"),
        P(None, "tensor"),
        P("tensor"),
        P("tensor"),
        P("tensor", None),
        P(),
        P(),
        P(),
        P(None, "tensor"),
        P("tensor"),
        P("tensor", None),
        P(),
        P(),
        P(),
        P(("dp", "ctx"), None),
    )
    out_specs = (
        P(("dp", "ctx"), None),
        P(("dp", "ctx"), None),
        P(None, "tensor"),
        P(None, "tensor"),
        P(None, "tensor"),
        P("tensor"),
        P("tensor"),
        P("tensor", None),
        P(),
        P(),
        P(),
        P(None, "tensor"),
        P("tensor"),
        P("tensor", None),
        P(),
        P(),
        P(),
    )
    return jax.shard_map(body, mesh=mesh, in_specs=in_specs, out_specs=out_specs, check_vma=False)
```

profile of v0, /device:TPU:0, one launch (start us, length us, event | category | flops | bytes accessed | tf_op | source)
XLA Modules:
  0.0 743.4 jit_solution(2113761524882374570)
XLA Ops:
  7.3 2.8 convolution_convert_fusion.4
  12.7 13.7 %all-gather = bf16[1,2048]{1,0:T(2,128)(2,1)S(1)} all-gather(bf16[1,512]{1,0:T(2,128)(2,1)S(1)} %get-tuple-element.288), channel_id=2, replica_groups=mesh['dp'=4,'ctx'=4,'tensor'=2] {'ctx'}, dimensions={1}, use_global_device_ids=true | all-gather | bytes 5120 | tf_op jit(solution)/shard_map/all_gather | solution.py:84
  29.1 21.0 %all-gather.4.cloned.1.call-done = bf16[2048,384]{1,0:T(8,128)(2,1)} async-done(((bf16[512,384]{1,0:T(8,128)(2,1)}), bf16[2048,384]{1,0:T(8,128)(2,1)}) %all-gather.4.cloned.1.call-update) | async-done | bytes 1572880 | tf_op jit(solution)/shard_map/all_gather | solution.py:82
  52.6 4.1 copy.45
  56.8 31.5 %all-gather.6.cloned.1.call-done = bf16[2048,384]{1,0:T(8,128)(2,1)} async-done(((bf16[512,384]{1,0:T(8,128)(2,1)}), bf16[2048,384]{1,0:T(8,128)(2,1)}) %all-gather.6.cloned.1.call-update) | async-done | bytes 1572880 | tf_op jit(solution)/shard_map/all_gather | solution.py:83
  90.8 4.1 copy.46
  94.9 38.4 %while.28 = (s32[]{:T(128)}, bf16[6,512,64]{1,2,0:T(8,128)(2,1)S(1)}, f32[6,512,1]{1,2,0:T(1,128)}, bf16[6,512,64]{2,1,0:T(8,128)(2,1)}, bf16[6,2048,64]{2,1,0:T...) while((s32[]{:T(128)}, ...), condition=%wide.region_3.4_spmd.clone, body=%wide.region_0.3_spmd.clone.sunk | while | flops 286260736 | bytes 13946985 | solution.py:111
  140.6 28.8 %all-reduce.8.cloned.1.call-done = bf16[512,768]{1,0:T(8,128)(2,1)} async-done(((bf16[512,768]{1,0:T(8,128)(2,1)}), bf16[512,768]{1,0:T(8,128)(2,1)}) %all-reduce.8.cloned.1.call-update) | async-done | bytes 786448 | tf_op jit(solution)/shard_map/psum | solution.py:113
  171.5 9.5 %multiply_convert_fusion.1 = (bf16[512,1536]{1,0:T(8,128)(2,1)S(1)}, f32[512,1536]{1,0:T(8,128)}, f32[512,1536]{1,0:T(8,128)}) fusion(f32[1536]{0:T(1024)S(1)} %copy-done.41, bf16[768,1536]{1,0:T(8,128)(2,1)S(1)} %copy-done, f32[768]{0:T(1024)S(1)} %copy-done.38, f32[768]{0:T(1024)S(1)} %copy-done.23, f32[512]{0:T(512)S(1)} %add_rsqrt_fusion.1, ...), kind=kOutput, calls=%fused_computation.62 | convolution fusion | flops 1263403008 | bytes 11815936 | tf_op jit(solution)/shard_map/dot_general | solution.py:14
  184.8 34.2 %all-reduce.10.cloned.1.call-done = bf16[512,768]{1,0:T(8,128)(2,1)} async-done(((bf16[512,768]{1,0:T(8,128)(2,1)}), bf16[512,768]{1,0:T(8,128)(2,1)}) %all-reduce.10.cloned.1.call-update) | async-done | bytes 786448 | tf_op jit(solution)/shard_map/psum | solution.py:126
  225.0 2.9 convert_reduce_fusion
  231.5 34.4 %all-reduce.12.cloned.1.call-done = bf16[512,768]{1,0:T(8,128)(2,1)} async-done(((bf16[512,768]{1,0:T(8,128)(2,1)}), bf16[512,768]{1,0:T(8,128)(2,1)}) %all-reduce.12.cloned.1.call-update) | async-done | bytes 786448 | tf_op jit(solution)/shard_map/psum | solution.py:145
  265.9 3.5 multiply_reduce_fusion.1
  273.7 70.0 %while.29 = (s32[]{:T(128)}, bf16[6,512,64]{1,2,0:T(8,128)(2,1)S(1)}, bf16[6,2048,64]{1,2,0:T(8,128)(2,1)}, bf16[6,2048,64]{1,2,0:T(8,128)(2,1)}, bf16[6,512,64]...) while((s32[]{:T(128)}, ...), condition=%wide.region_17.18_spmd.clone, body=%wide.region_15.17_spmd.clone.sunk | while | flops 681737728 | bytes 34759808 | solution.py:169
  345.1 5.1 fusion.67
  350.3 3.8 fusion.73
  357.4 21.8 %reduce-scatter.3.cloned.1.call-done = bf16[512,384]{0,1:T(8,128)(2,1)} async-done(((bf16[2048,384]{0,1:T(8,128)(2,1)}), bf16[512,384]{0,1:T(8,128)(2,1)}) %reduce-scatter.3.cloned.1.call-update) | async-done | bytes 393232 | tf_op jit(solution)/shard_map/reduce_scatter | solution.py:174
  379.1 3.0 fusion.82
  382.1 33.8 %reduce-scatter.5.cloned.1.call-done = bf16[512,384]{0,1:T(8,128)(2,1)} async-done(((bf16[2048,384]{0,1:T(8,128)(2,1)}), bf16[512,384]{0,1:T(8,128)(2,1)}) %reduce-scatter.5.cloned.1.call-update) | async-done | bytes 393232 | tf_op jit(solution)/shard_map/reduce_scatter | solution.py:177
  415.8 3.5 add_convert_fusion.1
  424.7 61.2 %all-reduce = (f32[384]{0:T(512)}, f32[384]{0:T(512)}, f32[768]{0:T(1024)}, f32[768]{0:T(1024)}, f32[768]{0:T(1024)}, /*index=5*/f32[1536]{0:T(1024)}, f32[768]{0:T(1024)}, f32[768]{0:T(1024)}, f32[768]{0:T(1024)}) all-reduce(f32[384]{0:T(512)S(1)} %reduce_sum.182, ...), channel_id=1, replica_groups=mesh['dp'=4,'ctx'=4,'tensor'=2] {'dp','ctx'}, use_global_device_ids=true, to_apply=%region_25.26 | all-reduce | flops 6912 | bytes 55296 | tf_op jit(solution)/shard_map/psum | solution.py:210
  488.3 231.7 %all-reduce.16.cloned.1.call-done = (f32[768,384]{0,1:T(8,128)}, f32[768,384]{0,1:T(8,128)}, f32[768,384]{0,1:T(8,128)}, f32[384,768]{1,0:T(8,128)}, f32[768,1536]{1,0:T(8,128)}, /*index=5*/f32[1536,768]{1,0:T(8,128)}) async-done(((f32[768,384]{0,1:T(8,128)}, f32[768,384]{0,1:T(8,128)}, f32[768,384]{0,1:T(8,128)}, f32[384,768]{1,0:T(8,128)}, f32[768,1536]{1,0:T(8,128)}, /*index=5*/f32[1536,768]{1,0:T(8,128)}), ...) | async-done | bytes 14155792 | tf_op jit(solution)/shard_map/psum | solution.py:210
  720.1 2.7 copy.50
  728.0 5.5 copy.92
  (259 shorter events, 166.2 us)
Async XLA Ops:
  7.2 164.2 %copy-start = (bf16[768,1536]{1,0:T(8,128)(2,1)S(1)}, bf16[768,1536]{1,0:T(8,128)(2,1)}, u32[]{:S(2)}) copy-start(bf16[768,1536]{1,0:T(8,128)(2,1)} %param.33) | copy-start | bytes 7077892
  7.2 42.8 %all-gather.4.cloned.1.call-start = ((), (), s32[]{:S(2)}) async-start(), calls=%async_computation.2 | async-start | bytes 1966080 | tf_op jit(solution)/shard_map/all_gather | solution.py:82
  10.1 78.1 %all-gather.6.cloned.1.call-start = ((), (), s32[]{:S(2)}) async-start(), calls=%async_computation.3 | async-start | bytes 1966080 | tf_op jit(solution)/shard_map/all_gather | solution.py:83
  12.6 156.8 %all-reduce.8.cloned.1.call-start = ((), (), s32[]{:S(2)}) async-start(), calls=%async_computation.4 | async-start | bytes 1572864 | tf_op jit(solution)/shard_map/psum | solution.py:113
  133.3 38.1 %copy-start.12 = (bf16[6,512,64]{1,2,0:T(8,128)(2,1)}, bf16[6,512,64]{1,2,0:T(8,128)(2,1)S(1)}, u32[]{:S(2)}) copy-start(bf16[6,512,64]{1,2,0:T(8,128)(2,1)S(1)} %get-tuple-element.109) | copy-start | bytes 1179652
  136.0 83.0 %all-reduce.10.cloned.1.call-start = ((), (), s32[]{:S(2)}) async-start(), calls=%async_computation.5 | async-start | bytes 1572864 | tf_op jit(solution)/shard_map/psum | solution.py:126
  170.9 10.1 %copy-start.26 = (f32[512]{0:T(512)}, f32[512]{0:T(512)S(1)}, u32[]{:S(2)}) copy-start(f32[512]{0:T(512)S(1)} %broadcast_multiply_fusion.5) | copy-start | bytes 6148
  171.5 9.6 %copy-start.29 = (f32[512]{0:T(512)}, f32[512]{0:T(512)S(1)}, u32[]{:S(2)}) copy-start(f32[512]{0:T(512)S(1)} %add_rsqrt_fusion.1) | copy-start | bytes 6148
  171.5 10.7 %copy-start.49 = (bf16[1536,768]{1,0:T(8,128)(2,1)S(1)}, bf16[1536,768]{1,0:T(8,128)(2,1)}, u32[]{:S(2)}) copy-start(bf16[1536,768]{1,0:T(8,128)(2,1)} %param.35) | copy-start | bytes 7077892
  182.2 36.8 %copy-start.24 = (f32[768]{0:T(1024)S(1)}, f32[768]{0:T(1024)}, u32[]{:S(2)}) copy-start(f32[768]{0:T(1024)} %convert_element_type.185) | copy-start | bytes 9220
  182.2 36.8 %copy-start.27 = (f32[512]{0:T(512)S(1)}, f32[512]{0:T(512)}, u32[]{:S(2)}) copy-start(f32[512]{0:T(512)} %copy-done.26) | copy-start | bytes 6148
  182.2 36.8 %copy-start.30 = (f32[512]{0:T(512)S(1)}, f32[512]{0:T(512)}, u32[]{:S(2)}) copy-start(f32[512]{0:T(512)} %copy-done.29) | copy-start | bytes 6148
  182.2 36.8 %copy-start.39 = (f32[768]{0:T(1024)S(1)}, f32[768]{0:T(1024)}, u32[]{:S(2)}) copy-start(f32[768]{0:T(1024)} %convert_element_type.186) | copy-start | bytes 9220
  184.5 81.4 %all-reduce.12.cloned.1.call-start = ((), (), s32[]{:S(2)}) async-start(), calls=%async_computation.6 | async-start | bytes 1572864 | tf_op jit(solution)/shard_map/psum | solution.py:145
  231.4 38.0 %copy-start.4 = (f32[512,768]{1,0:T(8,128)S(1)}, f32[512,768]{1,0:T(8,128)}, u32[]{:S(2)}) copy-start(f32[512,768]{1,0:T(8,128)} %copy-done.3) | copy-start | bytes 4718596
  231.4 38.0 %copy-start.9 = (bf16[512,768]{1,0:T(8,128)(2,1)S(1)}, bf16[512,768]{1,0:T(8,128)(2,1)}, u32[]{:S(2)}) copy-start(bf16[512,768]{1,0:T(8,128)(2,1)} %all-reduce.8.cloned.1.call-done) | copy-start | bytes 2359300
  231.4 147.7 %reduce-scatter.3.cloned.1.call-start = ((), (), s32[]{:S(2)}) async-start(), calls=%async_computation.7 | async-start | bytes 1966080 | tf_op jit(solution)/shard_map/reduce_scatter | solution.py:174
  343.7 72.2 %reduce-scatter.5.cloned.1.call-start = ((), (), s32[]{:S(2)}) async-start(), calls=%async_computation.8 | async-start | bytes 1966080 | tf_op jit(solution)/shard_map/reduce_scatter | solution.py:177
  344.4 5.8 copy-start.10
  344.4 5.8 copy-start.25
  344.5 141.4 %all-reduce.14.cloned.1.call-start = ((), (), s32[]{:S(2)}) async-start(), calls=%async_computation.9 | async-start | bytes 1572864 | tf_op jit(solution)/shard_map/psum | solution.py:193
  357.4 58.5 %copy-start.21 = (bf16[768,384]{1,0:T(8,128)(2,1)S(1)}, bf16[768,384]{1,0:T(8,128)(2,1)}, u32[]{:S(2)}) copy-start(bf16[768,384]{1,0:T(8,128)(2,1)} %param.26) | copy-start | bytes 1769476
  419.4 300.7 %all-reduce.16.cloned.1.call-start = ((), (), s32[]{:S(2)}) async-start(), calls=%async_computation.10 | async-start | bytes 28311552 | tf_op jit(solution)/shard_map/psum | solution.py:210
  727.0 6.5 slice-start
  (42 other events, 115.0 us)
Sparse Core Ops, SparseCore 0:
  10.2 39.8 all-gather.3
  52.2 35.9 all-gather.5
  136.1 33.1 all-reduce.7
  184.7 34.3 all-reduce.9
  231.5 34.3 all-reduce.11
  343.8 35.2 reduce-scatter.2
  381.5 34.2 reduce-scatter.4
  419.5 33.2 all-reduce.13
  459.1 260.8 all-reduce.15
where the time goes:
time: 746 us; the launch traced here: 743 us
  waiting for transfers between devices  438 us (59%)
  matrix products  141 us (19%)
  blocking collectives  74.9 us (10%)
  local copies, waits for them, and re-layouts  44.8 us (6%)
  other arithmetic  29.9 us (4%)
  between operations  14.4 us (2%)
    psum x1, waiting for transfers between devices, body(): lax.psum((query_grad, key_grad, value_grad, qbias_grad, vbias_grad, oproj...  232 us
    psum x1, blocking collectives, body(): lax.psum((query_grad, key_grad, value_grad, qbias_grad, vbias_grad, oproj...  61.2 us
    dot_general x24, matrix products, inner_cols(): lax.dot_general(left, right, contract_cols, preferred_element_type=jnp.fl...  52.3 us
    dot_general x18, matrix products, matmul(): return jnp.dot(left, right, preferred_element_type=jnp.float32)  47.6 us
    dot_general x18, matrix products, inner_rows(): lax.dot_general(left, right, contract_rows, preferred_element_type=jnp.fl...  40.7 us
    psum x1, waiting for transfers between devices, body(): lax.psum(inner_cols(grad_pre, expand_proj).astype(jnp.bfloat16), 'tensor')  34.4 us
    psum x1, waiting for transfers between devices, body(): lax.psum(matmul(hidden, shrink_proj).astype(jnp.bfloat16), 'tensor')  34.2 us
    reduce_scatter x1, waiting for transfers between devices, body(): lax.psum_scatter(join_heads(value_back).astype(jnp.bfloat16), 'ctx', scat...  33.8 us
  transfers between devices with their start and end apart: 9, of which 8 were waited for; matrix products, arithmetic and copies ran while one was open for 5% of the time, Pallas kernels for 0%

commit v1 on v0

--- a/solution.py
+++ b/solution.py
@@ -208,24 +208,27 @@
         fgain_grad,
         fshift_grad,
     ) = lax.psum(
-        (
-            query_grad,
-            key_grad,
-            value_grad,
-            qbias_grad,
-            vbias_grad,
-            oproj_grad,
-            obias_grad,
-            again_grad,
-            ashift_grad,
-            expand_grad,
-            ebias_grad,
-            shrink_grad,
-            sbias_grad,
-            fgain_grad,
-            fshift_grad,
+        lax.psum(
+            (
+                query_grad,
+                key_grad,
+                value_grad,
+                qbias_grad,
+                vbias_grad,
+                oproj_grad,
+                obias_grad,
+                again_grad,
+                ashift_grad,
+                expand_grad,
+                ebias_grad,
+                shrink_grad,
+                sbias_grad,
+                fgain_grad,
+                fshift_grad,
+            ),
+            "ctx",
         ),
-        ("dp", "ctx"),
+        "dp",
     )
     return (
         output.astype(jnp.bfloat16),

time: 746 us -> 1210 us (1.62)
  waiting for transfers between devices: 438 us -> 939 us
  blocking collectives: 74.9 us -> 42 us
    psum x0 -> x1, waiting for transfers between devices: none -> 248 us  [body(): lax.psum(lax.psum((query_grad, key_grad, value_grad, qbias_grad, vbias_gr...]
    psum x1, waiting for transfers between devices: 232 us -> 477 us  [body(): lax.psum((query_grad, key_grad, value_grad, qbias_grad, vbias_grad, oproj...]
    psum x1, blocking collectives: 61.2 us -> 17.3 us  [body(): lax.psum((query_grad, key_grad, value_grad, qbias_grad, vbias_grad, oproj...]
    reduce_scatter x1, waiting for transfers between devices: 21.8 us -> 34.2 us  [body(): lax.psum_scatter(join_heads(key_back).astype(jnp.bfloat16), 'ctx', scatte...]
    unnamed x122 -> x124, local copies, waits for them, and re-layouts: 29.6 us -> 30.2 us
  transfers between devices with their start and end apart: 9 -> 10, of which waited for: 8 -> 10; matrix products, arithmetic and copies ran while one was open for 5% -> 3% of each run, Pallas kernels for 0% -> 0%
where the time goes in v1:
time: 1210 us
  waiting for transfers between devices  939 us (78%)
  matrix products  138 us (11%)
  local copies, waits for them, and re-layouts  45.4 us (4%)
  blocking collectives  42 us (3%)
  other arithmetic  29.9 us (2%)
  between operations  14.9 us (1%)
    psum x1, waiting for transfers between devices, body(): lax.psum((query_grad, key_grad, value_grad, qbias_grad, vbias_grad, oproj...  477 us
    psum x1, waiting for transfers between devices, body(): lax.psum(lax.psum((query_grad, key_grad, value_grad, qbias_grad, vbias_gr...  248 us
    dot_general x24, matrix products, inner_cols(): lax.dot_general(left, right, contract_cols, preferred_element_type=jnp.fl...  48 us
    dot_general x18, matrix products, matmul(): return jnp.dot(left, right, preferred_element_type=jnp.float32)  47.5 us
    dot_general x18, matrix products, inner_rows(): lax.dot_general(left, right, contract_rows, preferred_element_type=jnp.fl...  42.6 us
    psum x1, waiting for transfers between devices, body(): lax.psum(inner_cols(grad_pre, expand_proj).astype(jnp.bfloat16), 'tensor')  34.4 us
    reduce_scatter x1, waiting for transfers between devices, body(): lax.psum_scatter(join_heads(key_back).astype(jnp.bfloat16), 'ctx', scatte...  34.2 us
    psum x1, waiting for transfers between devices, body(): lax.psum(matmul(hidden, shrink_proj).astype(jnp.bfloat16), 'tensor')  34.2 us
  transfers between devices with their start and end apart: 10, of which 10 were waited for; matrix products, arithmetic and copies ran while one was open for 3% of the time, Pallas kernels for 0%

profile of v1, /device:TPU:0, one launch (start us, length us, event | category | flops | bytes accessed | tf_op | source)
XLA Modules:
  0.0 1210.5 jit_solution(13787616428495004286)
XLA Ops:
  7.3 2.8 convolution_convert_fusion.4
  12.7 13.7 %all-gather = bf16[1,2048]{1,0:T(2,128)(2,1)S(1)} all-gather(bf16[1,512]{1,0:T(2,128)(2,1)S(1)} %get-tuple-element.303), channel_id=2, replica_groups=mesh['dp'=4,'ctx'=4,'tensor'=2] {'ctx'}, dimensions={1}, use_global_device_ids=true | all-gather | bytes 5120 | tf_op jit(solution)/shard_map/all_gather | solution.py:84
  29.1 21.0 %all-gather.4.cloned.1.call-done = bf16[2048,384]{1,0:T(8,128)(2,1)} async-done(((bf16[512,384]{1,0:T(8,128)(2,1)}), bf16[2048,384]{1,0:T(8,128)(2,1)}) %all-gather.4.cloned.1.call-update) | async-done | bytes 1572880 | tf_op jit(solution)/shard_map/all_gather | solution.py:82
  52.6 4.1 copy.45
  56.8 31.5 %all-gather.6.cloned.1.call-done = bf16[2048,384]{1,0:T(8,128)(2,1)} async-done(((bf16[512,384]{1,0:T(8,128)(2,1)}), bf16[2048,384]{1,0:T(8,128)(2,1)}) %all-gather.6.cloned.1.call-update) | async-done | bytes 1572880 | tf_op jit(solution)/shard_map/all_gather | solution.py:83
  90.8 4.1 copy.46
  94.9 38.4 %while.28 = (s32[]{:T(128)}, bf16[6,512,64]{1,2,0:T(8,128)(2,1)S(1)}, f32[6,512,1]{1,2,0:T(1,128)}, bf16[6,512,64]{2,1,0:T(8,128)(2,1)}, bf16[6,2048,64]{2,1,0:T...) while((s32[]{:T(128)}, ...), condition=%wide.region_3.4_spmd.clone, body=%wide.region_0.3_spmd.clone.sunk | while | flops 286260736 | bytes 13946985 | solution.py:111
  140.6 28.8 %all-reduce.11.cloned.1.call-done = bf16[512,768]{1,0:T(8,128)(2,1)} async-done(((bf16[512,768]{1,0:T(8,128)(2,1)}), bf16[512,768]{1,0:T(8,128)(2,1)}) %all-reduce.11.cloned.1.call-update) | async-done | bytes 786448 | tf_op jit(solution)/shard_map/psum | solution.py:113
  171.5 9.5 multiply_convert_fusion.1
  184.8 34.2 %all-reduce.13.cloned.1.call-done = bf16[512,768]{1,0:T(8,128)(2,1)} async-done(((bf16[512,768]{1,0:T(8,128)(2,1)}), bf16[512,768]{1,0:T(8,128)(2,1)}) %all-reduce.13.cloned.1.call-update) | async-done | bytes 786448 | tf_op jit(solution)/shard_map/psum | solution.py:126
  225.0 2.9 convert_reduce_fusion
  231.5 34.4 %all-reduce.15.cloned.1.call-done = bf16[512,768]{1,0:T(8,128)(2,1)} async-done(((bf16[512,768]{1,0:T(8,128)(2,1)}), bf16[512,768]{1,0:T(8,128)(2,1)}) %all-reduce.15.cloned.1.call-update) | async-done | bytes 786448 | tf_op jit(solution)/shard_map/psum | solution.py:145
  265.9 3.5 multiply_reduce_fusion.1
  273.7 69.9 %while.29 = (s32[]{:T(128)}, bf16[6,512,64]{1,2,0:T(8,128)(2,1)S(1)}, bf16[6,2048,64]{1,2,0:T(8,128)(2,1)}, bf16[6,2048,64]{1,2,0:T(8,128)(2,1)}, bf16[6,512,64]...) while((s32[]{:T(128)}, ...), condition=%wide.region_17.18_spmd.clone, body=%wide.region_15.17_spmd.clone.sunk | while | flops 681737728 | bytes 34759808 | solution.py:169
  345.0 5.1 fusion.67
  350.2 3.8 fusion.73
  357.2 21.8 %reduce-scatter.5.cloned.1.call-done = bf16[512,384]{0,1:T(8,128)(2,1)} async-done(((bf16[2048,384]{0,1:T(8,128)(2,1)}), bf16[512,384]{0,1:T(8,128)(2,1)}) %reduce-scatter.5.cloned.1.call-update) | async-done | bytes 393232 | tf_op jit(solution)/shard_map/reduce_scatter | solution.py:177
  381.5 34.2 %reduce-scatter.3.cloned.1.call-done = bf16[512,384]{0,1:T(8,128)(2,1)} async-done(((bf16[2048,384]{0,1:T(8,128)(2,1)}), bf16[512,384]{0,1:T(8,128)(2,1)}) %reduce-scatter.3.cloned.1.call-update) | async-done | bytes 393232 | tf_op jit(solution)/shard_map/reduce_scatter | solution.py:174
  422.4 477.3 %all-reduce.19.cloned.1.call-done = (f32[768,384]{0,1:T(8,128)}, f32[768,384]{0,1:T(8,128)}, f32[768,384]{0,1:T(8,128)}, f32[384,768]{1,0:T(8,128)}, f32[768,1536]{1,0:T(8,128)}, /*index=5*/f32[1536,768]{1,0:T(8,128)}) async-done(((f32[768,384]{0,1:T(8,128)}, f32[768,384]{0,1:T(8,128)}, f32[768,384]{0,1:T(8,128)}, f32[384,768]{1,0:T(8,128)}, f32[768,1536]{1,0:T(8,128)}, /*index=5*/f32[1536,768]{1,0:T(8,128)}), ...) | async-done | bytes 14155792 | tf_op jit(solution)/shard_map/psum | solution.py:211
  900.9 17.3 %all-reduce = (f32[384]{0:T(512)S(1)}, f32[384]{0:T(512)S(1)}, f32[768]{0:T(1024)S(1)}, f32[768]{0:T(1024)S(1)}, f32[768]{0:T(1024)S(1)}, /*index=5*/f32[1536]{0...) all-reduce(f32[384]{0:T(512)S(1)} %reduce_sum.182, ...), channel_id=1, replica_groups=mesh['dp'=4,'ctx'=4,'tensor'=2] {'ctx'}, use_global_device_ids=true, to_apply=%region_28.29 | all-reduce | flops 6912 | bytes 55296 | tf_op jit(solution)/shard_map/psum | solution.py:211
  918.2 11.1 all-reduce.2
  929.3 6.7 all-reduce.17.cloned.1.call-done
  938.4 248.5 %all-reduce.21.cloned.1.call-done = (f32[768,384]{0,1:T(8,128)}, f32[768,384]{0,1:T(8,128)}, f32[768,384]{0,1:T(8,128)}, f32[384,768]{1,0:T(8,128)}, f32[768,1536]{1,0:T(8,128)}, /*index=5*/f32[1536,768]{1,0:T(8,128)}) async-done(((f32[768,384]{0,1:T(8,128)}, f32[768,384]{0,1:T(8,128)}, f32[768,384]{0,1:T(8,128)}, f32[384,768]{1,0:T(8,128)}, f32[768,1536]{1,0:T(8,128)}, /*index=5*/f32[1536,768]{1,0:T(8,128)}), ...) | async-done | bytes 14155792 | tf_op jit(solution)/shard_map/psum | solution.py:210
  1194.7 5.5 copy.98
  (265 shorter events, 173.7 us)
Async XLA Ops:
  7.2 164.2 %copy-start = (bf16[768,1536]{1,0:T(8,128)(2,1)S(1)}, bf16[768,1536]{1,0:T(8,128)(2,1)}, u32[]{:S(2)}) copy-start(bf16[768,1536]{1,0:T(8,128)(2,1)} %param.33) | copy-start | bytes 7077892
  7.2 42.8 %all-gather.4.cloned.1.call-start = ((), (), s32[]{:S(2)}) async-start(), calls=%async_computation.2 | async-start | bytes 1966080 | tf_op jit(solution)/shard_map/all_gather | solution.py:82
  10.1 78.1 %all-gather.6.cloned.1.call-start = ((), (), s32[]{:S(2)}) async-start(), calls=%async_computation.3 | async-start | bytes 1966080 | tf_op jit(solution)/shard_map/all_gather | solution.py:83
  12.6 156.8 %all-reduce.11.cloned.1.call-start = ((), (), s32[]{:S(2)}) async-start(), calls=%async_computation.4 | async-start | bytes 1572864 | tf_op jit(solution)/shard_map/psum | solution.py:113
  133.3 38.1 %copy-start.13 = (bf16[6,512,64]{1,2,0:T(8,128)(2,1)}, bf16[6,512,64]{1,2,0:T(8,128)(2,1)S(1)}, u32[]{:S(2)}) copy-start(bf16[6,512,64]{1,2,0:T(8,128)(2,1)S(1)} %get-tuple-element.109) | copy-start | bytes 1179652
  136.0 83.0 %all-reduce.13.cloned.1.call-start = ((), (), s32[]{:S(2)}) async-start(), calls=%async_computation.5 | async-start | bytes 1572864 | tf_op jit(solution)/shard_map/psum | solution.py:126
  170.9 10.1 copy-start.27
  171.5 9.5 copy-start.30
  171.5 10.7 copy-start.50
  182.2 36.8 %copy-start.25 = (f32[768]{0:T(1024)S(1)}, f32[768]{0:T(1024)}, u32[]{:S(2)}) copy-start(f32[768]{0:T(1024)} %convert_element_type.185) | copy-start | bytes 9220
  182.2 36.8 %copy-start.28 = (f32[512]{0:T(512)S(1)}, f32[512]{0:T(512)}, u32[]{:S(2)}) copy-start(f32[512]{0:T(512)} %copy-done.27) | copy-start | bytes 6148
  182.2 36.8 %copy-start.31 = (f32[512]{0:T(512)S(1)}, f32[512]{0:T(512)}, u32[]{:S(2)}) copy-start(f32[512]{0:T(512)} %copy-done.30) | copy-start | bytes 6148
  182.2 36.8 %copy-start.40 = (f32[768]{0:T(1024)S(1)}, f32[768]{0:T(1024)}, u32[]{:S(2)}) copy-start(f32[768]{0:T(1024)} %convert_element_type.186) | copy-start | bytes 9220
  184.5 81.4 %all-reduce.15.cloned.1.call-start = ((), (), s32[]{:S(2)}) async-start(), calls=%async_computation.6 | async-start | bytes 1572864 | tf_op jit(solution)/shard_map/psum | solution.py:145
  231.4 38.0 %copy-start.4 = (f32[512,768]{1,0:T(8,128)S(1)}, f32[512,768]{1,0:T(8,128)}, u32[]{:S(2)}) copy-start(f32[512,768]{1,0:T(8,128)} %copy-done.3) | copy-start | bytes 4718596
  231.4 38.0 %copy-start.9 = (bf16[512,768]{1,0:T(8,128)(2,1)S(1)}, bf16[512,768]{1,0:T(8,128)(2,1)}, u32[]{:S(2)}) copy-start(bf16[512,768]{1,0:T(8,128)(2,1)} %all-reduce.11.cloned.1.call-done) | copy-start | bytes 2359300
  231.4 147.6 %reduce-scatter.5.cloned.1.call-start = ((), (), s32[]{:S(2)}) async-start(), calls=%async_computation.8 | async-start | bytes 1966080 | tf_op jit(solution)/shard_map/reduce_scatter | solution.py:177
  343.6 72.2 %reduce-scatter.3.cloned.1.call-start = ((), (), s32[]{:S(2)}) async-start(), calls=%async_computation.7 | async-start | bytes 1966080 | tf_op jit(solution)/shard_map/reduce_scatter | solution.py:174
  344.4 5.8 copy-start.10
  344.4 5.8 copy-start.26
  344.4 555.3 %all-reduce.19.cloned.1.call-start = ((), (), s32[]{:S(2)}) async-start(), calls=%async_computation.10 | async-start | bytes 28311552 | tf_op jit(solution)/shard_map/psum | solution.py:211
  418.3 517.7 %all-reduce.17.cloned.1.call-start = ((), (), s32[]{:S(2)}) async-start(), calls=%async_computation.9 | async-start | bytes 1572864 | tf_op jit(solution)/shard_map/psum | solution.py:193
  422.4 764.5 %all-reduce.21.cloned.1.call-start = ((), (), s32[]{:S(2)}) async-start(), calls=%async_computation.11 | async-start | bytes 28311552 | tf_op jit(solution)/shard_map/psum | solution.py:210
  1193.7 6.5 slice-start
  (44 other events, 118.8 us)
Sparse Core Ops, SparseCore 0:
  10.2 39.8 all-gather.3
  52.2 35.9 all-gather.5
  136.1 33.1 all-reduce.10
  184.6 34.3 all-reduce.12
  231.5 34.2 all-reduce.14
  343.7 35.2 reduce-scatter.4
  381.4 34.2 reduce-scatter.2
  420.5 479.1 all-reduce.18
  902.7 33.2 all-reduce.16
  938.9 247.8 all-reduce.20
